TPU v7x, 32 devices: a whole 2x2x4 slice. The times are simulated.
32 devices in a mesh: freq: 4 (over z), tm: 4 (over x, core), grp: 2 (over y).
Axes of the slice: x: 2, y: 2, z: 4, core: 2. Of those that a mesh axis runs over, the one named last changes fastest.
Arguments:
- voltages: bfloat16 [4, 2, 1024, 4096], P(None, None, ('freq', 'grp'), 'tm'), may hold values from -6 to 6
- prior_gains: float32 [4, 2, 1024], P('freq'), may hold values from -4.2 to 4.2
- station_flags: int32 [512], replicated, may hold values 0 or 1
- ingest_map: int32 [512], replicated, may hold values from 0 to 511, each once
- station_coords: float32 [2, 512], replicated, may hold values from -40 to 40
- pointing: int32 [2, 256], replicated, may hold values from 0 to 63
- corr_channels: int32 [4], replicated, may hold values from 0 to 3, each once
- beam_channels: int32 [4], replicated, may hold values from 0 to 3, each once
Outputs:
- visibilities: float32 [4, 2, 1024, 1024], P('freq', None, 'grp', 'tm')
- solved_gains: float32 [4, 2, 1024], P('freq')
- tied_beams: bfloat16 [4, 2, 2, 256, 4096], P('freq', None, None, 'grp', 'tm')
Inputs may be any that keep to these rules, and one draw needn't show every extreme that they name: `ingest_map`: each station appears in exactly one ingest slot. `corr_channels`: each channel is handled by exactly one correlator slot. `beam_channels`: each channel is handled by exactly one beamformer slot.
All inputs are finite; a program needn't handle non-finite values.
Results may differ from a plain program's by a relative error of at most 0.0049.
Values may be sent and summed in bfloat16 or wider, within the bound.
A program may use at most 64 MiB of HBM per device.

v0:
```python
import math
import jax
import jax.numpy as jnp
from jax import lax
from jax.sharding import PartitionSpec as P

S = 512
ITERS = 4
grid_cells = 64.0


def weights_for(gains_sel, ratio, pointing_part, slot_coords):
    east_dir = (pointing_part[0].astype(jnp.float32) + 0.5) / grid_cells - 0.5
    north_dir = (pointing_part[1].astype(jnp.float32) + 0.5) / grid_cells - 0.5
    phase = (
        2.0
        * math.pi
        * ratio
        * (
            east_dir[:, None] * slot_coords[0][None, :]
            + north_dir[:, None] * slot_coords[1][None, :]
        )
    )
    cosine = jnp.cos(phase)
    sine = jnp.sin(phase)
    gain_real = gains_sel[0].reshape(2, S)
    gain_imag = gains_sel[1].reshape(2, S)
    denom = jnp.maximum(gain_real * gain_real + gain_imag * gain_imag, 0.5)
    along_real = gain_real / denom
    along_imag = gain_imag / denom
    factor = 1.0 / math.sqrt(S)
    w_real = (cosine[None] * along_real[:, None, :] - sine[None] * along_imag[:, None, :]) * factor
    w_imag = -(cosine[None] * along_imag[:, None, :] + sine[None] * along_real[:, None, :]) * factor
    upper = jnp.stack([w_real, -w_imag], axis=2)
    lower = jnp.stack([w_imag, w_real], axis=2)
    return jnp.stack([upper, lower], axis=1).astype(jnp.bfloat16)


def body(
    voltages,
    prior_gains,
    station_flags,
    ingest_map,
    station_coords,
    pointing,
    corr_channels,
    beam_channels,
):
    highest = lax.Precision.HIGHEST
    n_freq = lax.axis_size("freq")
    n_time = lax.axis_size("tm")
    n_group = lax.axis_size("grp")
    freq_index = lax.axis_index("freq")
    time_index = lax.axis_index("tm")
    group_index = lax.axis_index("grp")
    channels_all = voltages.shape[0]
    per_device = channels_all // n_freq
    per_input = voltages.shape[2]
    samples = voltages.shape[3]
    inputs_all = 2 * S
    corr_source = jnp.take(voltages, corr_channels, axis=0)
    beam_source = jnp.take(voltages, beam_channels, axis=0)
    corr_half, beam_half = (
        lax.all_to_all(corr_source, "freq", split_axis=0, concat_axis=2, tiled=True),
        lax.all_to_all(beam_source, "freq", split_axis=0, concat_axis=2, tiled=True),
    )
    split_shape = (per_device, 2, n_freq, per_input, samples)
    corr_pair, beam_pair = (
        lax.all_gather(corr_half.reshape(split_shape), "grp", axis=3, tiled=True),
        lax.all_gather(beam_half.reshape(split_shape), "grp", axis=3, tiled=True),
    )
    full_shape = (per_device, 2, inputs_all, samples)
    corr_volts = corr_pair.reshape(full_shape)
    beam_volts = beam_pair.reshape(full_shape)
    slot_keep = 1 - jnp.take(station_flags, ingest_map)
    keep = jnp.concatenate([slot_keep, slot_keep]).astype(jnp.bfloat16)
    corr_volts = corr_volts * keep[None, None, :, None]
    beam_volts = beam_volts * keep[None, None, :, None]
    rows = inputs_all // n_group
    row_start = group_index * rows
    mine = lax.dynamic_slice_in_dim(corr_volts, row_start, rows, 2)
    left = jnp.stack([mine, jnp.stack([mine[:, 1], -mine[:, 0]], axis=1)], axis=1)
    partial_value = jnp.einsum(
        "corit,crjt->coij", left, corr_volts, preferred_element_type=jnp.float32
    )
    partial_value = partial_value * (1.0 / (samples * n_time))
    columns = inputs_all // n_time
    vis_block = lax.psum_scatter(partial_value, "tm", scatter_dimension=3, tiled=True)
    gains = prior_gains
    for iteration in range(ITERS):
        power = jnp.sum(gains * gains, axis=(1, 2)) + 1e-06
        along = lax.dynamic_slice_in_dim(gains, time_index * columns, columns, 2)
        real_real = jnp.einsum("cij,cj->ci", vis_block[:, 0], along[:, 0], precision=highest)
        imag_imag = jnp.einsum("cij,cj->ci", vis_block[:, 1], along[:, 1], precision=highest)
        real_imag = jnp.einsum("cij,cj->ci", vis_block[:, 0], along[:, 1], precision=highest)
        imag_real = jnp.einsum("cij,cj->ci", vis_block[:, 1], along[:, 0], precision=highest)
        update = jnp.stack([real_real - imag_imag, imag_real + real_imag], axis=1)
        update = lax.psum(update, "tm")
        own_rows = lax.dynamic_slice_in_dim(gains, row_start, rows, 2)
        fresh = 0.5 * (own_rows + inputs_all * update / power[:, None, None])
        gains = lax.all_gather(fresh, "grp", axis=2, tiled=True)
    all_gains = lax.all_gather(gains, "freq", axis=0, tiled=True)
    my_beam = lax.dynamic_slice_in_dim(beam_channels, freq_index * per_device, per_device, 0)
    onehot = (corr_channels[None, :] == my_beam[:, None]).astype(jnp.float32)
    selected = jnp.einsum("ck,kri->cri", onehot, all_gains, precision=highest)
    ratio = 0.875 + 0.25 * (my_beam.astype(jnp.float32) + 0.5) / channels_all
    beams_mine = pointing.shape[1] // n_group
    pointing_part = lax.dynamic_slice_in_dim(pointing, group_index * beams_mine, beams_mine, 1)
    slot_coords = jnp.take(station_coords, ingest_map, axis=1)
    weights = jax.vmap(weights_for, in_axes=(0, 0, None, None))(
        selected, ratio, pointing_part, slot_coords
    )
    block = beam_volts.reshape(per_device, 2, 2, S, samples)
    beams = jnp.einsum("cpobrq,crpqt->cpobt", weights, block, preferred_element_type=jnp.float32)
    return (vis_block, gains, beams.astype(jnp.bfloat16))


def solution(mesh):
    return jax.shard_map(
        body,
        mesh=mesh,
        in_specs=(
            P(None, None, ("freq", "grp"), "tm"),
            P("freq", None, None),
            P(),
            P(),
            P(),
            P(),
            P(),
            P(),
        ),
        out_specs=(
            P("freq", None, "grp", "tm"),
            P("freq", None, None),
            P("freq", None, None, "grp", "tm"),
        ),
        check_vma=False,
    )
```

profile of v0, /device:TPU:0, one launch (start us, length us, event | category | flops | bytes accessed | tf_op | source)
XLA Modules:
  0.0 313.8 jit_solution(3851320219780948037)
XLA Ops:
  7.2 0.8 compare_select_fusion.1
  8.0 0.7 compare_and_fusion
  8.8 2.0 gather_fusion.2
  10.8 1.9 broadcast_select_fusion.1
  12.7 54.4 %all_to_all.30 = bf16[4,2,128,1024]{3,2,1,0:T(8,128)(2,1)} all-to-all(bf16[4,2,128,1024]{3,2,1,0:T(8,128)(2,1)S(1)} %broadcast_select_fusion.1), channel_id=1, replica_groups=mesh['freq'=4,'tm'=4,'grp'=2] {'freq'}, dimensions={0} | all-to-all | bytes 4194304 | tf_op jit(solution)/shard_map/all_to_all | solution.py:64
  67.2 2.0 gather_fusion.3
  69.2 1.9 broadcast_select_fusion
  71.1 50.7 %all_to_all.31 = bf16[4,2,128,1024]{3,2,1,0:T(8,128)(2,1)} all-to-all(bf16[4,2,128,1024]{3,2,1,0:T(8,128)(2,1)S(1)} %broadcast_select_fusion), channel_id=1, replica_groups=mesh['freq'=4,'tm'=4,'grp'=2] {'freq'}, dimensions={0} | all-to-all | bytes 4194304 | tf_op jit(solution)/shard_map/all_to_all | solution.py:65
  121.8 0.6 copy-done.5
  122.5 3.5 %gather_fusion = s32[512]{0:T(512)S(1)} fusion(s32[512]{0:T(512)S(1)} %copy-done.1, s32[1024]{0:T(1024)S(1)} %pad_clamp_fusion.1), kind=kCustom, calls=%fused_computation.2 | custom fusion | bytes 6144 | tf_op jit(solution)/shard_map/jit(_take)/gather | solution.py:75
  126.0 0.1 dynamic-slice
  126.1 2.5 broadcast_multiply_fusion
  128.7 0.4 copy.24
  129.1 1.8 copy-done.3
  131.0 0.4 copy.23
  131.4 0.4 dynamic-slice_multiply_fusion
  131.8 0.1 fusion.74
  132.0 0.2 maximum_bitcast_fusion.4
  132.2 0.4 fusion.76
  132.6 6.1 %fusion.5 = f32[1,2,512,1024]{3,2,1,0:T(8,128)} fusion(bf16[2,1024,1024,1]{2,1,0,3:T(8,128)(2,1)S(1)} %bitcast.171, bf16[1,1,2,512,1024]{4,3,2,1,0:T(8,128)(2,1)S(1)} %maximum_bitcast_fusion.4, bf16[1,1,2,512,1024]{4,3,2,1,0:T(8,128)(2,1)S(1)} %fusion.76), kind=kOutput, calls=%fused_computation.11 | convolution fusion | flops 4298113024 | bytes 12582912 | tf_op jit(solution)/shard_map/corit,crjt->coij/dot_general | solution.py:83
  138.8 0.6 copy-done.8
  139.4 0.6 dynamic_slice.42
  140.0 0.1 copy.25
  140.1 1.0 gather_fusion.1
  141.8 0.6 multiply_reduce_fusion.3
  143.1 0.1 select_bitcast_fusion
  143.2 0.3 slice_reduce_fusion.1
  143.5 1.8 fusion.32
  145.3 36.2 %all-gather.5.cloned.1.call-done = bf16[1,2,4,256,1024]{4,3,1,2,0:T(8,128)(2,1)} async-done(((bf16[1,2,4,128,1024]{4,3,1,2,0:T(8,128)(2,1)}), bf16[1,2,4,256,1024]{4,3,1,2,0:T(8,128)(2,1)}) %all-gather.5.cloned.1.call-update) | async-done | bytes 4194320 | tf_op jit(solution)/shard_map/all_gather | solution.py:70
  181.6 4.6 %copy.27 = bf16[1,2,4,256,1024]{4,3,2,1,0:T(8,128)(2,1)} copy(bf16[1,2,4,256,1024]{4,3,1,2,0:T(8,128)(2,1)} %all-gather.5.cloned.1.call-done) | data formatting | bytes 8388608 | tf_op jit(solution)/shard_map/all_gather | solution.py:70
  186.2 42.9 %reduce-scatter.2.cloned.1.call-done = f32[1,2,512,256]{3,2,1,0:T(8,128)} async-done(((f32[1,2,512,1024]{3,2,1,0:T(8,128)}), f32[1,2,512,256]{3,2,1,0:T(8,128)}) %reduce-scatter.2.cloned.1.call-update) | async-done | bytes 1048592 | tf_op jit(solution)/shard_map/reduce_scatter | solution.py:88
  229.1 1.7 fusion.29
  230.8 1.6 fusion.21
  232.4 1.6 fusion.22
  234.0 1.6 fusion.30
  235.6 5.8 %psum.28 = f32[1,2,512]{2,1,0:T(2,128)S(1)} all-reduce(f32[1,2,512]{2,1,0:T(2,128)S(1)} %pad_maximum_fusion), channel_id=1, replica_groups=mesh['freq'=4,'tm'=4,'grp'=2] {'tm'}, use_global_device_ids=true, to_apply=%region_1.3 | all-reduce | flops 1024 | bytes 8192 | tf_op jit(solution)/shard_map/psum | solution.py:98
  241.4 4.4 %all_gather.22 = f32[1,2,1024]{2,1,0:T(2,128)S(1)} all-gather(f32[1,2,512]{2,1,0:T(2,128)S(1)} %fusion.38), channel_id=1, replica_groups=mesh['freq'=4,'tm'=4,'grp'=2] {'grp'}, dimensions={2}, use_global_device_ids=true | all-gather | bytes 12288 | tf_op jit(solution)/shard_map/all_gather | solution.py:101
  245.8 0.6 multiply_reduce_fusion.2
  246.4 0.5 fusion.27
  246.9 0.6 fusion.19
  247.5 0.6 fusion.20
  248.0 0.6 fusion.28
  248.6 5.7 %psum.29 = f32[1,2,512]{2,1,0:T(2,128)S(1)} all-reduce(f32[1,2,512]{2,1,0:T(2,128)S(1)} %pad_maximum_fusion.1), channel_id=1, replica_groups=mesh['freq'=4,'tm'=4,'grp'=2] {'tm'}, use_global_device_ids=true, to_apply=%region_3.5 | all-reduce | flops 1024 | bytes 8192 | tf_op jit(solution)/shard_map/psum | solution.py:98
  255.0 4.5 %all_gather.23 = f32[1,2,1024]{2,1,0:T(2,128)S(1)} all-gather(f32[1,2,512]{2,1,0:T(2,128)S(1)} %fusion.39), channel_id=1, replica_groups=mesh['freq'=4,'tm'=4,'grp'=2] {'grp'}, dimensions={2}, use_global_device_ids=true | all-gather | bytes 12288 | tf_op jit(solution)/shard_map/all_gather | solution.py:101
  259.5 0.6 multiply_reduce_fusion.1
  260.1 0.5 fusion.25
  260.6 0.6 fusion.17
  261.2 0.6 fusion.18
  261.8 0.6 fusion.26
  262.4 5.7 %psum.30 = f32[1,2,512]{2,1,0:T(2,128)S(1)} all-reduce(f32[1,2,512]{2,1,0:T(2,128)S(1)} %pad_maximum_fusion.2), channel_id=1, replica_groups=mesh['freq'=4,'tm'=4,'grp'=2] {'tm'}, use_global_device_ids=true, to_apply=%region_5.7 | all-reduce | flops 1024 | bytes 8192 | tf_op jit(solution)/shard_map/psum | solution.py:98
  268.7 4.4 %all_gather.24 = f32[1,2,1024]{2,1,0:T(2,128)S(1)} all-gather(f32[1,2,512]{2,1,0:T(2,128)S(1)} %fusion.40), channel_id=1, replica_groups=mesh['freq'=4,'tm'=4,'grp'=2] {'grp'}, dimensions={2}, use_global_device_ids=true | all-gather | bytes 12288 | tf_op jit(solution)/shard_map/all_gather | solution.py:101
  273.1 0.6 multiply_reduce_fusion
  273.7 0.5 fusion.23
  274.2 0.6 fusion.15
  274.8 0.6 fusion.16
  275.3 0.6 fusion.24
  275.9 5.7 %psum.31 = f32[1,2,512]{2,1,0:T(2,128)S(1)} all-reduce(f32[1,2,512]{2,1,0:T(2,128)S(1)} %pad_maximum_fusion.3), channel_id=1, replica_groups=mesh['freq'=4,'tm'=4,'grp'=2] {'tm'}, use_global_device_ids=true, to_apply=%region_7.9 | all-reduce | flops 1024 | bytes 8192 | tf_op jit(solution)/shard_map/psum | solution.py:98
  282.3 4.4 %all_gather.25 = f32[1,2,1024]{2,1,0:T(2,128)S(1)} all-gather(f32[1,2,512]{2,1,0:T(2,128)S(1)} %fusion.41), channel_id=1, replica_groups=mesh['freq'=4,'tm'=4,'grp'=2] {'grp'}, dimensions={2}, use_global_device_ids=true | all-gather | bytes 12288 | tf_op jit(solution)/shard_map/all_gather | solution.py:101
  286.6 13.4 %all_gather.26 = f32[4,2,1024]{2,1,0:T(2,128)S(1)} all-gather(f32[1,2,1024]{2,1,0:T(2,128)S(1)} %all_gather.25), channel_id=1, replica_groups=mesh['freq'=4,'tm'=4,'grp'=2] {'freq'}, dimensions={0}, use_global_device_ids=true | all-gather | bytes 40960 | tf_op jit(solution)/shard_map/all_gather | solution.py:102
  300.0 0.8 fusion.33
  300.9 1.1 negate_convert_fusion
  302.0 0.1 maximum_bitcast_fusion.5
  302.1 4.6 %fusion.8 = bf16[1,2,2,128,1024]{4,3,2,1,0:T(8,128)(2,1)} fusion(bf16[2,1,128,2,512]{4,2,3,1,0:T(8,128)(2,1)S(1)} %get-tuple-element.17, bf16[2,1,128,2,512]{4,2,3,1,0:T(8,128)(2,1)S(1)} %get-tuple-element.16, bf16[2,2,512,1024]{3,2,1,0:T(8,128)(2,1)} %bitcast.170, bf16[2,512]{1,0:T(2,128)(2,1)S(1)} %convert_element_type.50), kind=kOutput, calls=%fused_computation.19 | convolution fusion | flops 1076887552 | bytes 6293504 | tf_op jit(solution)/shard_map/cpobrq,crpqt->cpobt/dot_general | solution.py:114
  306.6 0.6 copy.47
  (55 shorter events, 0.6 us)
Async XLA Ops:
  7.2 1.6 copy-start
  7.2 118.9 %all-gather.3.cloned.1.call-start = ((), (), s32[]{:S(2)}) async-start(), calls=%async_computation.3 | async-start | bytes 6291456 | tf_op jit(solution)/shard_map/all_gather | solution.py:69
  67.2 114.4 %all-gather.5.cloned.1.call-start = ((), (), s32[]{:S(2)}) async-start(), calls=%async_computation.5 | async-start | bytes 6291456 | tf_op jit(solution)/shard_map/all_gather | solution.py:70
  121.8 0.7 copy-start.5
  121.8 0.7 copy-start.1
  121.8 107.3 %reduce-scatter.2.cloned.1.call-start = ((), (), s32[]{:S(2)}) async-start(), calls=%async_computation.4 | async-start | bytes 5242880 | tf_op jit(solution)/shard_map/reduce_scatter | solution.py:88
  128.7 2.3 copy-start.3
  138.7 0.7 copy-start.8
  138.7 1.3 copy-start.7
  138.7 3.1 copy-start.4
  138.7 4.3 %copy-start.9 = (s32[2,256]{1,0:T(2,128)S(1)}, s32[2,256]{1,0:T(2,128)}, u32[]{:S(2)}) copy-start(s32[2,256]{1,0:T(2,128)} %param.15) | copy-start | bytes 6148
  229.1 17.3 %copy-start.2 = (f32[1,2,512,256]{3,2,1,0:T(8,128)S(1)}, f32[1,2,512,256]{3,2,1,0:T(8,128)}, u32[]{:S(2)}) copy-start(f32[1,2,512,256]{3,2,1,0:T(8,128)} %reduce-scatter.2.cloned.1.call-done) | copy-start | bytes 3145732
  260.1 39.9 %copy-start.6 = (s32[4]{0:T(128)S(1)}, s32[4]{0:T(128)}, u32[]{:S(2)}) copy-start(s32[4]{0:T(128)} %param.16) | copy-start | bytes 52
Sparse Core Ops, SparseCore 0:
  67.3 55.9 all-gather.2
  124.8 56.7 all-gather.4
  184.7 44.3 reduce-scatter.1
where the time goes:
time: 315 us; the launch traced here: 314 us
  blocking collectives  159 us (50%)
  waiting for transfers between devices  79.2 us (25%)
  matrix products  24.5 us (8%)
  local copies, waits for them, and re-layouts  19 us (6%)
  between operations  17.3 us (5%)
  other arithmetic  14.7 us (5%)
    all_to_all x1, blocking collectives, body(): lax.all_to_all(corr_source, 'freq', split_axis=0, concat_axis=2, tiled=True)  54.4 us
    all_to_all x1, blocking collectives, body(): lax.all_to_all(beam_source, 'freq', split_axis=0, concat_axis=2, tiled=True)  50.7 us
    reduce_scatter x1, waiting for transfers between devices, body(): lax.psum_scatter(partial_value, 'tm', scatter_dimension=3, tiled=True)  42.9 us
    all_gather x1, waiting for transfers between devices, body(): lax.all_gather(beam_half.reshape(split_shape), 'grp', axis=3, tiled=True)  36.2 us
    psum x4, blocking collectives, body(): update = lax.psum(update, 'tm')  22.8 us
    all_gather x4, blocking collectives, body(): gains = lax.all_gather(fresh, 'grp', axis=2, tiled=True)  17.6 us
    all_gather x1, blocking collectives, body(): all_gains = lax.all_gather(gains, 'freq', axis=0, tiled=True)  13.4 us
  transfers between devices with their start and end apart: 3, of which 2 were waited for; matrix products, arithmetic and copies ran while one was open for 9% of the time, Pallas kernels for 0%

commit v1 on v0

--- a/solution.py
+++ b/solution.py
@@ -62,7 +62,12 @@
     beam_source = jnp.take(voltages, beam_channels, axis=0)
     corr_half, beam_half = (
         lax.all_to_all(corr_source, "freq", split_axis=0, concat_axis=2, tiled=True),
-        lax.all_to_all(beam_source, "freq", split_axis=0, concat_axis=2, tiled=True),
+        jnp.concatenate(
+            lax.all_to_all(
+                jnp.stack(jnp.split(beam_source, lax.axis_size("freq"), axis=0)), "freq", 0, 0
+            ),
+            axis=2,
+        ),
     )
     split_shape = (per_device, 2, n_freq, per_input, samples)
     corr_pair, beam_pair = (

time: 315 us -> 285 us (0.905)
  blocking collectives: 159 us -> 110 us
  waiting for transfers between devices: 79.2 us -> 94.1 us
  starting transfers between devices: 0.12 us -> 4.86 us
    all_gather x1, waiting for transfers between devices: 0.01 us -> 51.8 us  [body(): lax.all_gather(corr_half.reshape(split_shape), 'grp', axis=3, tiled=True)]
    all_to_all x1 -> x0, blocking collectives: 50.7 us -> none  [body(): lax.all_to_all(beam_source, 'freq', split_axis=0, concat_axis=2, tiled=True)]
    reduce_scatter x1, waiting for transfers between devices: 42.9 us -> 0.02 us  [body(): lax.psum_scatter(partial_value, 'tm', scatter_dimension=3, tiled=True)]
    all_to_all x0 -> x1, waiting for transfers between devices: none -> 42.2 us  [body(): lax.all_to_all(jnp.stack(jnp.split(beam_source, lax.axis_size('freq'), ax...]
    all_gather x1, waiting for transfers between devices: 36.2 us -> 0.02 us  [body(): lax.all_gather(beam_half.reshape(split_shape), 'grp', axis=3, tiled=True)]
    all_to_all x0 -> x1, starting transfers between devices: none -> 4.77 us  [body(): lax.all_to_all(jnp.stack(jnp.split(beam_source, lax.axis_size('freq'), ax...]
    all_gather x1 -> x0, local copies, waits for them, and re-layouts: 4.6 us -> none  [body(): lax.all_gather(beam_half.reshape(split_shape), 'grp', axis=3, tiled=True)]
    all_to_all x0 -> x1, local copies, waits for them, and re-layouts: none -> 3.15 us  [body(): lax.all_to_all(jnp.stack(jnp.split(beam_source, lax.axis_size('freq'), ax...]
  transfers between devices with their start and end apart: 3 -> 4, of which waited for: 2 -> 2; matrix products, arithmetic and copies ran while one was open for 9% -> 12% of each run, Pallas kernels for 0% -> 0%
where the time goes in v1:
time: 285 us; the launch traced here: 284 us
  blocking collectives  110 us (39%)
  waiting for transfers between devices  94.1 us (33%)
  matrix products  24.7 us (9%)
  local copies, waits for them, and re-layouts  19.3 us (7%)
  between operations  17.4 us (6%)
  other arithmetic  14.1 us (5%)
  starting transfers between devices  4.86 us (2%)
    all_to_all x1, blocking collectives, body(): lax.all_to_all(corr_source, 'freq', split_axis=0, concat_axis=2, tiled=True)  54.4 us
    all_gather x1, waiting for transfers between devices, body(): lax.all_gather(corr_half.reshape(split_shape), 'grp', axis=3, tiled=True)  51.8 us
    all_to_all x1, waiting for transfers between devices, body(): lax.all_to_all(jnp.stack(jnp.split(beam_source, lax.axis_size('freq'), ax...  42.2 us
    psum x4, blocking collectives, body(): update = lax.psum(update, 'tm')  23.9 us
    all_gather x4, blocking collectives, body(): gains = lax.all_gather(fresh, 'grp', axis=2, tiled=True)  18.2 us
    all_gather x1, blocking collectives, body(): all_gains = lax.all_gather(gains, 'freq', axis=0, tiled=True)  13.1 us
    dot_general x1, matrix products, body(): jnp.einsum('corit,crjt->coij', left, corr_volts, preferred_element_type=j...  6.11 us
  transfers between devices with their start and end apart: 4, of which 2 were waited for; matrix products, arithmetic and copies ran while one was open for 12% of the time, Pallas kernels for 0%

profile of v1, /device:TPU:0, one launch (start us, length us, event | category | flops | bytes accessed | tf_op | source)
XLA Modules:
  0.0 284.2 jit_solution(13020526652034354769)
XLA Ops:
  7.2 0.8 compare_select_fusion.1
  8.0 0.7 compare_and_fusion
  8.8 2.0 gather_fusion.2
  10.8 1.9 broadcast_select_fusion.1
  12.7 54.4 %all_to_all.20 = bf16[4,2,128,1024]{3,2,1,0:T(8,128)(2,1)} all-to-all(bf16[4,2,128,1024]{3,2,1,0:T(8,128)(2,1)S(1)} %broadcast_select_fusion.1), channel_id=1, replica_groups=mesh['freq'=4,'tm'=4,'grp'=2] {'freq'}, dimensions={0} | all-to-all | bytes 4194304 | tf_op jit(solution)/shard_map/all_to_all | solution.py:64
  67.2 0.6 copy-done.5
  67.8 3.5 %gather_fusion = s32[512]{0:T(512)S(1)} fusion(s32[512]{0:T(512)S(1)} %copy-done.1, s32[1024]{0:T(1024)S(1)} %pad_clamp_fusion.1), kind=kCustom, calls=%fused_computation.2 | custom fusion | bytes 6144 | tf_op jit(solution)/shard_map/jit(_take)/gather | solution.py:80
  71.4 0.1 dynamic-slice
  71.5 51.8 %all-gather.3.cloned.1.call-done = bf16[1,2,4,256,1024]{4,3,1,2,0:T(8,128)(2,1)} async-done(((bf16[1,2,4,128,1024]{4,3,1,2,0:T(8,128)(2,1)}), bf16[1,2,4,256,1024]{4,3,1,2,0:T(8,128)(2,1)}) %all-gather.3.cloned.1.call-update) | async-done | bytes 4194320 | tf_op jit(solution)/shard_map/all_gather | solution.py:74
  123.3 2.6 copy.28
  125.9 0.4 dynamic-slice_multiply_fusion
  126.3 0.4 fusion.76
  126.7 1.8 copy-done.3
  128.5 0.3 broadcast_multiply_fusion
  128.9 0.4 copy.29
  129.3 0.1 fusion.74
  129.4 0.2 maximum_bitcast_fusion.4
  129.7 6.1 %fusion.5 = f32[1,2,512,1024]{3,2,1,0:T(8,128)} fusion(bf16[2,1024,1024,1]{2,1,0,3:T(8,128)(2,1)S(1)} %bitcast.178, bf16[1,1,2,512,1024]{4,3,2,1,0:T(8,128)(2,1)S(1)} %maximum_bitcast_fusion.4, bf16[1,1,2,512,1024]{4,3,2,1,0:T(8,128)(2,1)S(1)} %fusion.76), kind=kOutput, calls=%fused_computation.11 | convolution fusion | flops 4298113024 | bytes 12582912 | tf_op jit(solution)/shard_map/corit,crjt->coij/dot_general | solution.py:88
  135.8 2.0 gather_fusion.3
  137.8 1.9 broadcast_select_fusion
  139.7 0.2 slice_bitcast_fusion.3
  139.8 1.6 pad_maximum_fusion
  141.5 4.8 %all-to-all-start.1 = ((bf16[4,1,2,128,1024]{4,3,2,1,0:T(8,128)(2,1)}), bf16[4,1,2,128,1024]{4,3,2,1,0:T(8,128)(2,1)}, u32[]{:S(2)}, u32[]{:S(2)}) async-start(bf16[4,1,2,128,1024]{4,3,2,1,0:T(8,128)(2,1)} %pad_maximum_fusion), calls=%async_computation.2 | async-start | bytes 4194304 | tf_op jit(solution)/shard_map/all_to_all | solution.py:66
  146.3 0.6 dynamic_slice.42
  146.9 0.1 copy.30
  147.1 1.0 gather_fusion.1
  148.8 0.6 multiply_reduce_fusion.3
  150.1 0.1 select_bitcast_fusion
  150.2 0.3 slice_reduce_fusion.1
  150.6 1.8 fusion.32
  152.4 42.2 %all-to-all-done.1 = bf16[4,1,2,128,1024]{4,3,2,1,0:T(8,128)(2,1)} async-done(((bf16[4,1,2,128,1024]{4,3,2,1,0:T(8,128)(2,1)}), bf16[4,1,2,128,1024]{4,3,2,1,0:T(8,128)(2,1)}, u32[]{:S(2)}, u32[]{:S(2)}) %all-to-all-start.1) | async-done | bytes 2097184 | tf_op jit(solution)/shard_map/all_to_all | solution.py:66
  194.6 3.2 %copy.52 = bf16[4,1,2,128,1024]{4,3,0,2,1:T(8,128)(2,1)} copy(bf16[4,1,2,128,1024]{4,3,2,1,0:T(8,128)(2,1)} %all-to-all-done.1) | data formatting | bytes 4194304 | tf_op jit(solution)/shard_map/all_to_all | solution.py:66
  197.8 1.7 fusion.29
  199.5 1.6 fusion.21
  201.1 1.7 fusion.22
  202.7 1.7 fusion.30
  204.5 5.7 %psum.28 = f32[1,2,512]{2,1,0:T(2,128)S(1)} all-reduce(f32[1,2,512]{2,1,0:T(2,128)S(1)} %pad_maximum_fusion.1), channel_id=1, replica_groups=mesh['freq'=4,'tm'=4,'grp'=2] {'tm'}, use_global_device_ids=true, to_apply=%region_1.3 | all-reduce | flops 1024 | bytes 8192 | tf_op jit(solution)/shard_map/psum | solution.py:103
  210.1 4.6 %all_gather.22 = f32[1,2,1024]{2,1,0:T(2,128)S(1)} all-gather(f32[1,2,512]{2,1,0:T(2,128)S(1)} %fusion.38), channel_id=1, replica_groups=mesh['freq'=4,'tm'=4,'grp'=2] {'grp'}, dimensions={2}, use_global_device_ids=true | all-gather | bytes 12288 | tf_op jit(solution)/shard_map/all_gather | solution.py:106
  214.7 0.5 fusion.27
  215.3 0.6 fusion.19
  215.8 0.6 fusion.20
  216.4 0.6 fusion.28
  216.9 0.6 multiply_reduce_fusion.2
  218.2 6.1 %psum.29 = f32[1,2,512]{2,1,0:T(2,128)S(1)} all-reduce(f32[1,2,512]{2,1,0:T(2,128)S(1)} %pad_maximum_fusion.2), channel_id=1, replica_groups=mesh['freq'=4,'tm'=4,'grp'=2] {'tm'}, use_global_device_ids=true, to_apply=%region_3.5 | all-reduce | flops 1024 | bytes 8192 | tf_op jit(solution)/shard_map/psum | solution.py:103
  224.3 4.8 %all_gather.23 = f32[1,2,1024]{2,1,0:T(2,128)S(1)} all-gather(f32[1,2,512]{2,1,0:T(2,128)S(1)} %fusion.39), channel_id=1, replica_groups=mesh['freq'=4,'tm'=4,'grp'=2] {'grp'}, dimensions={2}, use_global_device_ids=true | all-gather | bytes 12288 | tf_op jit(solution)/shard_map/all_gather | solution.py:106
  229.1 0.6 multiply_reduce_fusion.1
  230.3 0.5 fusion.25
  230.9 0.6 fusion.17
  231.5 0.6 fusion.18
  232.0 0.6 fusion.26
  232.6 6.1 %psum.30 = f32[1,2,512]{2,1,0:T(2,128)S(1)} all-reduce(f32[1,2,512]{2,1,0:T(2,128)S(1)} %pad_maximum_fusion.3), channel_id=1, replica_groups=mesh['freq'=4,'tm'=4,'grp'=2] {'tm'}, use_global_device_ids=true, to_apply=%region_5.7 | all-reduce | flops 1024 | bytes 8192 | tf_op jit(solution)/shard_map/psum | solution.py:103
  238.7 4.6 %all_gather.24 = f32[1,2,1024]{2,1,0:T(2,128)S(1)} all-gather(f32[1,2,512]{2,1,0:T(2,128)S(1)} %fusion.40), channel_id=1, replica_groups=mesh['freq'=4,'tm'=4,'grp'=2] {'grp'}, dimensions={2}, use_global_device_ids=true | all-gather | bytes 12288 | tf_op jit(solution)/shard_map/all_gather | solution.py:106
  243.3 0.6 multiply_reduce_fusion
  244.5 0.5 fusion.23
  245.1 0.6 fusion.15
  245.6 0.6 fusion.16
  246.2 0.6 fusion.24
  246.8 6.1 %psum.31 = f32[1,2,512]{2,1,0:T(2,128)S(1)} all-reduce(f32[1,2,512]{2,1,0:T(2,128)S(1)} %pad_maximum_fusion.4), channel_id=1, replica_groups=mesh['freq'=4,'tm'=4,'grp'=2] {'tm'}, use_global_device_ids=true, to_apply=%region_7.9 | all-reduce | flops 1024 | bytes 8192 | tf_op jit(solution)/shard_map/psum | solution.py:103
  252.8 4.4 %all_gather.25 = f32[1,2,1024]{2,1,0:T(2,128)S(1)} all-gather(f32[1,2,512]{2,1,0:T(2,128)S(1)} %fusion.41), channel_id=1, replica_groups=mesh['freq'=4,'tm'=4,'grp'=2] {'grp'}, dimensions={2}, use_global_device_ids=true | all-gather | bytes 12288 | tf_op jit(solution)/shard_map/all_gather | solution.py:106
  257.2 13.1 %all_gather.26 = f32[4,2,1024]{2,1,0:T(2,128)S(1)} all-gather(f32[1,2,1024]{2,1,0:T(2,128)S(1)} %all_gather.25), channel_id=1, replica_groups=mesh['freq'=4,'tm'=4,'grp'=2] {'freq'}, dimensions={0}, use_global_device_ids=true | all-gather | bytes 40960 | tf_op jit(solution)/shard_map/all_gather | solution.py:107
  270.3 0.8 fusion.33
  271.2 1.1 negate_convert_fusion
  272.5 4.5 %fusion.8 = bf16[1,2,2,128,1024]{4,3,2,1,0:T(8,128)(2,1)} fusion(bf16[2,1,128,2,512]{4,2,3,1,0:T(8,128)(2,1)S(1)} %get-tuple-element.21, bf16[2,1,128,2,512]{4,2,3,1,0:T(8,128)(2,1)S(1)} %get-tuple-element.20, bf16[2,2,512,1024]{3,2,1,0:T(8,128)(2,1)} %bitcast.204, bf16[2,512]{1,0:T(2,128)(2,1)S(1)} %convert_element_type.50), kind=kOutput, calls=%fused_computation.21 | convolution fusion | flops 1076887552 | bytes 6293504 | tf_op jit(solution)/shard_map/cpobrq,crpqt->cpobt/dot_general | solution.py:119
  277.1 0.6 copy.54
  (58 shorter events, 0.7 us)
Async XLA Ops:
  7.2 1.6 copy-start
  7.2 116.1 %all-gather.3.cloned.1.call-start = ((), (), s32[]{:S(2)}) async-start(), calls=%async_computation.3 | async-start | bytes 6291456 | tf_op jit(solution)/shard_map/all_gather | solution.py:74
  67.1 0.7 copy-start.5
  67.1 0.7 copy-start.1
  67.2 130.6 %reduce-scatter.2.cloned.1.call-start = ((), (), s32[]{:S(2)}) async-start(), calls=%async_computation.4 | async-start | bytes 5242880 | tf_op jit(solution)/shard_map/reduce_scatter | solution.py:93
  126.3 2.2 copy-start.3
  141.5 4.8 %copy-start.8 = (s32[4]{0:T(128)S(1)}, s32[4]{0:T(128)}, u32[]{:S(2)}) copy-start(s32[4]{0:T(128)} %param.17) | copy-start | bytes 52
  141.5 5.5 %copy-start.7 = (f32[2,512]{1,0:T(2,128)S(1)}, f32[2,512]{1,0:T(2,128)}, u32[]{:S(2)}) copy-start(f32[2,512]{1,0:T(2,128)} %param.14) | copy-start | bytes 12292
  141.5 7.3 %copy-start.4 = (f32[1,2,1024]{2,1,0:T(2,128)S(1)}, f32[1,2,1024]{2,1,0:T(2,128)}, u32[]{:S(2)}) copy-start(f32[1,2,1024]{2,1,0:T(2,128)} %param.11) | copy-start | bytes 24580
  141.5 8.6 %copy-start.9 = (s32[2,256]{1,0:T(2,128)S(1)}, s32[2,256]{1,0:T(2,128)}, u32[]{:S(2)}) copy-start(s32[2,256]{1,0:T(2,128)} %param.15) | copy-start | bytes 6148
  141.5 53.1 %all-to-all-start.1 = ((bf16[4,1,2,128,1024]{4,3,2,1,0:T(8,128)(2,1)}), bf16[4,1,2,128,1024]{4,3,2,1,0:T(8,128)(2,1)}, u32[]{:S(2)}, u32[]{:S(2)}) async-start(bf16[4,1,2,128,1024]{4,3,2,1,0:T(8,128)(2,1)} %pad_maximum_fusion), calls=%async_computation.2 | async-start | bytes 4194304 | tf_op jit(solution)/shard_map/all_to_all | solution.py:66
  146.2 126.3 %all-gather.5.cloned.1.call-start = ((), (), s32[]{:S(2)}) async-start(), calls=%async_computation.5 | async-start | bytes 6291456 | tf_op jit(solution)/shard_map/all_gather | solution.py:75
  197.8 16.9 %copy-start.2 = (f32[1,2,512,256]{3,2,1,0:T(8,128)S(1)}, f32[1,2,512,256]{3,2,1,0:T(8,128)}, u32[]{:S(2)}) copy-start(f32[1,2,512,256]{3,2,1,0:T(8,128)} %reduce-scatter.2.cloned.1.call-done) | copy-start | bytes 3145732
  230.3 40.0 %copy-start.6 = (s32[4]{0:T(128)S(1)}, s32[4]{0:T(128)}, u32[]{:S(2)}) copy-start(s32[4]{0:T(128)} %param.16) | copy-start | bytes 52
Sparse Core Ops, SparseCore 0:
  67.3 55.9 all-gather.2
  135.9 44.3 reduce-scatter.1
  197.9 54.9 all-gather.4
